TPU v7x, 256 devices: a whole 4x4x8 slice. The times are simulated.
256 devices in a mesh: dist: 2 (over core), rows: 128 (over y, z, x).
Axes of the slice: x: 4, y: 4, z: 8, core: 2. Of those that a mesh axis runs over, the one named last changes fastest.
Arguments:
- holograms: bfloat16 [1, 4, 4, 1024, 1024], P(None, None, 'dist', 'rows'), may hold values from -6 to 6
- propagation: float32 [4], replicated, may hold values from 100 to 1000
- weights: bfloat16 [4, 1024, 1024], P(None, None, 'dist'), may hold values from -0.09375 to 0.09375
- angle_order: int32 [1, 4], replicated, may hold values from 0 to 3, each once within a row
- slab_rows: int32 [128], replicated, may hold values from 0 to 16, as said below
Outputs:
- slab: bfloat16 [2048, 1024], P('rows', 'dist')
Inputs may be any that keep to these rules, and one draw needn't show every extreme that they name: Owners 2j and 2j+1 together own 16 slices: slab_rows[2j] + slab_rows[2j+1] = 16, so owner 2j holds slices 2j 8 onward and owner 2j+1 the rest of that pair's range; in every draw some owner holds 16.
All inputs are finite; a program needn't handle non-finite values.
Results may differ from a plain program's by a relative error of at most 0.02.
Values may be sent and summed in bfloat16 or wider, within the bound.
A program may use at most 128 MiB of HBM per device.

v0:
```python
import math
import jax
import jax.numpy as jnp
from jax import lax
from jax.sharding import PartitionSpec as P

absorb_ratio = 0.1
regularizer = 0.05


def swapped(value, axis, bit):
    mask = 2**bit
    pairs = [(source, source ^ mask) for source in range(lax.axis_size(axis))]
    return lax.ppermute(value, axis, pairs)


def dft_tables(length):
    index = jnp.arange(length, dtype=jnp.int32)
    product = index[:, None] * index[None, :] % length
    turned = product.astype(jnp.float32) * (2.0 * math.pi / length)
    factor = 1.0 / math.sqrt(length)
    return (
        (jnp.cos(turned) * factor).astype(jnp.bfloat16),
        (jnp.sin(turned) * factor).astype(jnp.bfloat16),
    )


def on_device(holograms, propagation, weights, angle_order, slab_rows):
    mbatch, angles, dist_dev, rows_dev, width = holograms.shape
    groups = lax.axis_size("rows")
    capacity = 2 * rows_dev
    cosine, sine = dft_tables(width)
    col_cos = cosine.reshape(groups, rows_dev, width)
    col_sin = sine.reshape(groups, rows_dev, width)
    index = jnp.arange(width, dtype=jnp.int32)
    signed = jnp.where(index < width // 2, index, index - width).astype(jnp.float32)
    device = lax.axis_index("rows")
    local_freq = lax.dynamic_slice_in_dim(signed, device * rows_dev, rows_dev, 0)
    radius = (local_freq[:, None] ** 2 + signed[None, :] ** 2) / float(width * width)
    chirp = propagation[:, None, None] * radius[None]
    transfer = 2.0 * (jnp.sin(chirp) + absorb_ratio * jnp.cos(chirp))
    denom = jnp.sum(transfer * transfer, axis=0) + regularizer
    mine = lax.dynamic_slice_in_dim(transfer, lax.axis_index("dist") * dist_dev, dist_dev, 0)
    parity = device % 2
    offset = parity * slab_rows[device - parity]
    count = slab_rows[device]
    slot = jnp.arange(capacity, dtype=jnp.int32)[:, None]
    source = jnp.arange(capacity, dtype=jnp.int32)[None, :]
    select = ((source == offset + slot) & (slot < count)).astype(jnp.float32)
    flat = holograms[0].reshape(angles * dist_dev * rows_dev, width)
    row_re = jnp.dot(flat, cosine, preferred_element_type=jnp.float32).astype(jnp.bfloat16)
    row_im = (-jnp.dot(flat, sine, preferred_element_type=jnp.float32)).astype(jnp.bfloat16)
    row_re = row_re.reshape(angles * dist_dev, rows_dev, width)
    row_im = row_im.reshape(angles * dist_dev, rows_dev, width)
    pieces = (
        lax.all_to_all(row_re, "rows", split_axis=2, concat_axis=2, tiled=True),
        lax.all_to_all(row_im, "rows", split_axis=2, concat_axis=2, tiled=True),
    )
    items = pieces[0].shape[0]
    real_part = pieces[0].reshape(items, rows_dev, groups, rows_dev)
    imag_part = pieces[1].reshape(items, rows_dev, groups, rows_dev)
    out_re = jnp.einsum("aysk,syq->akq", real_part, col_cos, preferred_element_type=jnp.float32)
    out_re = out_re + jnp.einsum(
        "aysk,syq->akq", imag_part, col_sin, preferred_element_type=jnp.float32
    )
    out_im = jnp.einsum("aysk,syq->akq", imag_part, col_cos, preferred_element_type=jnp.float32)
    out_im = out_im - jnp.einsum(
        "aysk,syq->akq", real_part, col_sin, preferred_element_type=jnp.float32
    )
    spec_re = out_re
    spec_im = out_im
    spec_re = spec_re.reshape(angles, dist_dev, rows_dev, width)
    spec_im = spec_im.reshape(angles, dist_dev, rows_dev, width)
    numer_re = jnp.sum(mine[None] * spec_re, axis=1)
    numer_im = jnp.sum(mine[None] * spec_im, axis=1)
    numer_re, numer_im = (
        lax.psum(numer_re.astype(jnp.bfloat16), "dist").astype(jnp.float32),
        lax.psum(numer_im.astype(jnp.bfloat16), "dist").astype(jnp.float32),
    )
    spec_phase_re = (numer_re / denom).astype(jnp.bfloat16)
    spec_phase_im = (numer_im / denom).astype(jnp.bfloat16)
    half_re = jnp.einsum("akq,qy->aky", spec_phase_re, cosine, preferred_element_type=jnp.float32)
    half_re = (
        half_re - jnp.einsum("akq,qy->aky", spec_phase_im, sine, preferred_element_type=jnp.float32)
    ).astype(jnp.bfloat16)
    half_im = jnp.einsum("akq,qy->aky", spec_phase_im, cosine, preferred_element_type=jnp.float32)
    half_im = (
        half_im + jnp.einsum("akq,qy->aky", spec_phase_re, sine, preferred_element_type=jnp.float32)
    ).astype(jnp.bfloat16)
    pieces = (
        lax.all_to_all(half_re, "rows", split_axis=2, concat_axis=2, tiled=True),
        lax.all_to_all(half_im, "rows", split_axis=2, concat_axis=2, tiled=True),
    )
    items = pieces[0].shape[0]
    real_part = pieces[0].reshape(items, rows_dev, groups, rows_dev)
    imag_part = pieces[1].reshape(items, rows_dev, groups, rows_dev)
    result = jnp.einsum("aksy,skx->ayx", real_part, col_cos, preferred_element_type=jnp.float32)
    phase = (
        result - jnp.einsum("aksy,skx->ayx", imag_part, col_sin, preferred_element_type=jnp.float32)
    ).astype(jnp.bfloat16)
    chosen = weights[0 + angle_order[0]]
    partner = swapped(phase, "rows", 0)
    lower = jnp.where(parity == 1, partner, phase)
    upper = jnp.where(parity == 1, phase, partner)
    paired = jnp.concatenate([lower, upper], axis=1)
    rows_in = jnp.einsum(
        "ij,ajx->aix", select.astype(jnp.bfloat16), paired, preferred_element_type=jnp.float32
    ).astype(jnp.bfloat16)
    recon = jnp.einsum("ayx,axp->yp", rows_in, chosen, preferred_element_type=jnp.float32)
    return recon.astype(jnp.bfloat16)


def solution(mesh):
    return jax.shard_map(
        on_device,
        mesh=mesh,
        in_specs=(P(None, None, "dist", "rows", None), P(), P(None, None, "dist"), P(), P()),
        out_specs=P("rows", "dist"),
        check_vma=False,
    )
```

profile of v0, /device:TPU:2, one launch (start us, length us, event | category | flops | bytes accessed | tf_op | source)
XLA Modules:
  0.0 350.8 jit_solution(18105776519220072496)
XLA Ops:
  7.4 16.1 %fusion.66 = bf16[8,8,1024]{2,1,0:T(8,128)(2,1)S(1)} fusion(bf16[64,1024]{1,0:T(8,128)(2,1)S(1)} %bitcast.132), kind=kOutput, calls=%fused_computation.56 | convolution fusion | flops 151126016 | bytes 262144 | tf_op jit(solution)/shard_map/dot_general | solution.py:52
  25.1 2.9 reshape.156
  28.0 15.8 %all-to-all-start.1 = ((bf16[128,2,256]{2,1,0:T(2,128)(2,1)}), bf16[128,2,256]{2,1,0:T(2,128)(2,1)S(1)}, u32[]{:S(2)}, u32[]{:S(2)}) async-start(bf16[128,2,256]{2,1,0:T(2,128)(2,1)} %reshape.156), calls=%async_computation.1 | async-start | bytes 262144 | tf_op jit(solution)/shard_map/all_to_all | solution.py:57
  43.8 16.0 %fusion.65 = bf16[8,8,1024]{2,1,0:T(8,128)(2,1)S(1)} fusion(bf16[64,1024]{1,0:T(8,128)(2,1)S(1)} %bitcast.133), kind=kOutput, calls=%fused_computation.55 | convolution fusion | flops 151060480 | bytes 262144 | tf_op jit(solution)/shard_map/dot_general | solution.py:51
  61.3 2.9 reshape.154
  65.0 13.8 %all-to-all-start = ((bf16[128,2,256]{2,1,0:T(2,128)(2,1)}), bf16[128,2,256]{2,1,0:T(2,128)(2,1)S(1)}, u32[]{:S(2)}, u32[]{:S(2)}) async-start(bf16[128,2,256]{2,1,0:T(2,128)(2,1)} %reshape.154), calls=%async_computation | async-start | bytes 262144 | tf_op jit(solution)/shard_map/all_to_all | solution.py:56
  78.8 3.5 reshape.157
  82.3 4.3 %copy.30 = bf16[8,8,128,8]{3,2,1,0:T(8,128)(2,1)S(1)} copy(bf16[8,8,128,8]{1,0,3,2:T(8,128)(2,1)} %bitcast.136) | data formatting | bytes 262144 | tf_op jit(solution)/shard_map/reshape | solution.py:61
  86.6 3.6 %all-to-all-done = bf16[128,2,256]{2,1,0:T(2,128)(2,1)S(1)} async-done(((bf16[128,2,256]{2,1,0:T(2,128)(2,1)}), bf16[128,2,256]{2,1,0:T(2,128)(2,1)S(1)}, u32[]{:S(2)}, u32[]{:S(2)}) %all-to-all-start) | async-done | bytes 131104 | tf_op jit(solution)/shard_map/all_to_all | solution.py:56
  90.3 3.5 reshape.155
  93.7 5.4 %copy.28 = bf16[8,8,128,8]{3,2,1,0:T(8,128)(2,1)} copy(bf16[8,8,128,8]{1,0,3,2:T(8,128)(2,1)} %bitcast.137) | data formatting | bytes 262144 | tf_op jit(solution)/shard_map/reshape | solution.py:60
  99.1 16.0 %fusion.39 = f32[8,8,1024]{2,1,0:T(8,128)S(1)} fusion(bf16[8,8,128,8]{3,2,1,0:T(8,128)(2,1)S(1)} %copy.30, s32[128,8]{0,1:T(8,128)S(1)} %multiply_add_fusion), kind=kOutput, calls=%fused_computation.42 | convolution fusion | flops 150994944 | bytes 397312 | tf_op jit(solution)/shard_map/aysk,syq->akq/dot_general | solution.py:66
  115.2 16.1 %fusion.36 = f32[8,8,1024]{2,1,0:T(8,128)S(1)} fusion(bf16[8,8,128,8]{3,2,1,0:T(8,128)(2,1)S(1)} %copy-done.1, s32[128,8]{0,1:T(8,128)S(1)} %multiply_add_fusion), kind=kOutput, calls=%fused_computation.41 | convolution fusion | flops 150994944 | bytes 397312 | tf_op jit(solution)/shard_map/aysk,syq->akq/dot_general | solution.py:62
  131.2 16.5 %fusion.48 = f32[8,8,1024]{2,1,0:T(8,128)S(1)} fusion(f32[8,8,1024]{2,1,0:T(8,128)S(1)} %fusion.39, bf16[8,8,128,8]{3,2,1,0:T(8,128)(2,1)S(1)} %copy-done.1, s32[128,8]{0,1:T(8,128)S(1)} %multiply_add_fusion), kind=kOutput, calls=%fused_computation.45 | convolution fusion | flops 151060480 | bytes 659456 | tf_op jit(solution)/shard_map/aysk,syq->akq/dot_general | solution.py:67
  147.8 16.8 %multiply_reduce_fusion.1 = (bf16[4,8,1024]{2,1,0:T(8,128)(2,1)}, bf16[4,8,1024]{2,1,0:T(8,128)(2,1)}) fusion(f32[2,8,1024]{2,1,0:T(8,128)S(1)} %constant_dynamic-slice_fusion, f32[8,8,1024]{2,1,0:T(8,128)S(1)} %fusion.48, f32[8,8,1024]{2,1,0:T(8,128)S(1)} %fusion.36, bf16[8,8,128,8]{3,2,1,0:T(8,128)(2,1)S(1)} %copy.30, s32[128,8]{0,1:T(8,128)S(1)} %multiply_add_fusion), kind=kOutput, calls=%fused_computation.66 | convolution fusion | flops 151257088 | bytes 856064 | tf_op jit(solution)/shard_map/aysk,syq->akq/dot_general | solution.py:63
  164.6 26.7 %all-reduce.3.cloned.1.call-done = (bf16[4,8,1024]{2,1,0:T(8,128)(2,1)}, bf16[4,8,1024]{2,1,0:T(8,128)(2,1)}) async-done(((bf16[4,8,1024]{2,1,0:T(8,128)(2,1)}, bf16[4,8,1024]{2,1,0:T(8,128)(2,1)}), (bf16[4,8,1024]{2,1,0:T(8,128)(2,1)}, bf16[4,8,1024]{2,1,0:T(8,128)(2,1)})) %all-reduce.3.cloned.1.call-update) | async-done | bytes 131088 | tf_op jit(solution)/shard_map/psum | solution.py:78
  191.3 16.9 %fusion.14 = f32[4,8,1024]{2,1,0:T(8,128)S(1)} fusion(bf16[4,8,1024]{2,1,0:T(8,128)(2,1)} %get-tuple-element.8, f32[8,1024]{1,0:T(8,128)S(1)} %broadcast_add_fusion), kind=kOutput, calls=%fused_computation.25 | convolution fusion | flops 83984384 | bytes 229376 | tf_op jit(solution)/shard_map/akq,qy->aky/dot_general | solution.py:88
  208.2 16.1 %fusion.16 = f32[4,8,1024]{2,1,0:T(8,128)S(1)} fusion(bf16[4,8,1024]{2,1,0:T(8,128)(2,1)S(1)} %copy-done.5, f32[8,1024]{1,0:T(8,128)S(1)} %broadcast_add_fusion), kind=kOutput, calls=%fused_computation.27 | convolution fusion | flops 83984384 | bytes 229376 | tf_op jit(solution)/shard_map/akq,qy->aky/dot_general | solution.py:84
  224.3 15.9 %fusion.79 = bf16[4,8,1024]{2,1,0:T(8,128)(2,1)S(1)} fusion(f32[4,8,1024]{2,1,0:T(8,128)S(1)} %fusion.14, bf16[4,8,1024]{2,1,0:T(8,128)(2,1)S(1)} %copy-done.5, f32[8,1024]{1,0:T(8,128)S(1)} %broadcast_add_fusion), kind=kOutput, calls=%fused_computation.61 | convolution fusion | flops 84049920 | bytes 294912 | tf_op jit(solution)/shard_map/akq,qy->aky/dot_general | solution.py:86
  240.9 1.7 reshape.160
  242.6 14.3 %all-to-all-start.3 = ((bf16[128,2,128]{2,1,0:T(2,128)(2,1)}), bf16[128,2,128]{2,1,0:T(2,128)(2,1)S(1)}, u32[]{:S(2)}, u32[]{:S(2)}) async-start(bf16[128,2,128]{2,1,0:T(2,128)(2,1)} %reshape.160), calls=%async_computation.3 | async-start | bytes 131072 | tf_op jit(solution)/shard_map/all_to_all | solution.py:92
  257.0 15.9 %fusion.82 = bf16[4,8,1024]{2,1,0:T(8,128)(2,1)S(1)} fusion(f32[4,8,1024]{2,1,0:T(8,128)S(1)} %fusion.16, bf16[4,8,1024]{2,1,0:T(8,128)(2,1)S(1)} %copy-done.4, f32[8,1024]{1,0:T(8,128)S(1)} %broadcast_add_fusion), kind=kOutput, calls=%fused_computation.62 | convolution fusion | flops 84049920 | bytes 294912 | tf_op jit(solution)/shard_map/akq,qy->aky/dot_general | solution.py:82
  273.6 1.7 reshape.158
  275.3 13.8 %all-to-all-start.2 = ((bf16[128,2,128]{2,1,0:T(2,128)(2,1)}), bf16[128,2,128]{2,1,0:T(2,128)(2,1)S(1)}, u32[]{:S(2)}, u32[]{:S(2)}) async-start(bf16[128,2,128]{2,1,0:T(2,128)(2,1)} %reshape.158), calls=%async_computation.2 | async-start | bytes 131072 | tf_op jit(solution)/shard_map/all_to_all | solution.py:91
  290.3 5.0 %gather_fusion = bf16[4,1024,512]{2,1,0:T(8,128)(2,1)} fusion(bf16[4,1024,512]{2,1,0:T(8,128)(2,1)} %param.7, s32[1024]{0:T(1024)S(1)} %pad_clamp_fusion), kind=kCustom, calls=%fused_computation | custom fusion | bytes 8388624 | tf_op jit(solution)/shard_map/gather | solution.py:101
  296.4 2.1 copy.38
  298.5 1.8 all-to-all-done.2
  301.4 2.2 copy.36
  303.7 15.8 %fusion.57 = f32[4,8,1024]{2,1,0:T(8,128)S(1)} fusion(bf16[4,8,128,8]{3,2,1,0:T(8,128)(2,1)S(1)} %copy.36, s32[128,8]{0,1:T(8,128)S(1)} %multiply_add_fusion), kind=kOutput, calls=%fused_computation.51 | convolution fusion | flops 83886080 | bytes 200704 | tf_op jit(solution)/shard_map/aksy,skx->ayx/dot_general | solution.py:97
  319.5 16.0 %fusion.76 = bf16[4,8,1024]{2,1,0:T(8,128)(2,1)S(1)} fusion(f32[4,8,1024]{2,1,0:T(8,128)S(1)} %fusion.57, bf16[4,8,128,8]{3,2,1,0:T(8,128)(2,1)S(1)} %copy.38, s32[128,8]{0,1:T(8,128)S(1)} %multiply_add_fusion), kind=kOutput, calls=%fused_computation.60 | convolution fusion | flops 83951616 | bytes 266240 | tf_op jit(solution)/shard_map/aksy,skx->ayx/dot_general | solution.py:99
  337.7 2.2 collective-permute-done
  339.9 3.6 %fusion.86 = bf16[16,512]{1,0:T(8,128)(2,1)} fusion(bf16[4,1024,512]{2,1,0:T(8,128)(2,1)} %gather_fusion, bf16[4,8,1024]{2,1,0:T(8,128)(2,1)S(1)} %get-tuple-element.10, bf16[4,8,1024]{2,1,0:T(8,128)(2,1)S(1)} %get-tuple-element.9, s32[16]{0:T(128)S(1)} %iota_add_fusion, pred[16]{0:T(512)(128)(4,1)S(1)} %iota_compare_fusion.1), kind=kOutput, calls=%fused_computation.64 | convolution fusion | flops 69542912 | bytes 4341840 | tf_op jit(solution)/shard_map/ayx,axp->yp/dot_general | solution.py:109
  (39 shorter events, 11.2 us)
Async XLA Ops:
  6.5 0.9 copy-start
  28.0 37.0 %all-to-all-start.1 = ((bf16[128,2,256]{2,1,0:T(2,128)(2,1)}), bf16[128,2,256]{2,1,0:T(2,128)(2,1)S(1)}, u32[]{:S(2)}, u32[]{:S(2)}) async-start(bf16[128,2,256]{2,1,0:T(2,128)(2,1)} %reshape.156), calls=%async_computation.1 | async-start | bytes 262144 | tf_op jit(solution)/shard_map/all_to_all | solution.py:57
  59.7 4.6 %copy-start.3 = (f32[4]{0:T(128)S(1)}, f32[4]{0:T(128)}, u32[]{:S(2)}) copy-start(f32[4]{0:T(128)} %param.6) | copy-start | bytes 52
  65.0 25.3 %all-to-all-start = ((bf16[128,2,256]{2,1,0:T(2,128)(2,1)}), bf16[128,2,256]{2,1,0:T(2,128)(2,1)S(1)}, u32[]{:S(2)}, u32[]{:S(2)}) async-start(bf16[128,2,256]{2,1,0:T(2,128)(2,1)} %reshape.154), calls=%async_computation | async-start | bytes 262144 | tf_op jit(solution)/shard_map/all_to_all | solution.py:56
  78.8 112.5 %all-reduce.3.cloned.1.call-start = ((), (), s32[]{:S(2)}) async-start(), calls=%async_computation.4 | async-start | bytes 262144 | tf_op jit(solution)/shard_map/psum | solution.py:78
  99.1 16.0 %copy-start.1 = (bf16[8,8,128,8]{3,2,1,0:T(8,128)(2,1)S(1)}, bf16[8,8,128,8]{3,2,1,0:T(8,128)(2,1)}, u32[]{:S(2)}) copy-start(bf16[8,8,128,8]{3,2,1,0:T(8,128)(2,1)} %copy.28) | copy-start | bytes 393220
  131.2 33.4 %copy-start.6 = (s32[1,4]{1,0:T(1,128)S(1)}, s32[1,4]{1,0:T(1,128)}, u32[]{:S(2)}) copy-start(s32[1,4]{1,0:T(1,128)} %param.8) | copy-start | bytes 52
  191.3 16.9 %copy-start.5 = (bf16[4,8,1024]{2,1,0:T(8,128)(2,1)S(1)}, bf16[4,8,1024]{2,1,0:T(8,128)(2,1)}, u32[]{:S(2)}) copy-start(bf16[4,8,1024]{2,1,0:T(8,128)(2,1)} %get-tuple-element.7) | copy-start | bytes 196612
  224.3 32.6 %copy-start.4 = (bf16[4,8,1024]{2,1,0:T(8,128)(2,1)S(1)}, bf16[4,8,1024]{2,1,0:T(8,128)(2,1)}, u32[]{:S(2)}) copy-start(bf16[4,8,1024]{2,1,0:T(8,128)(2,1)} %get-tuple-element.8) | copy-start | bytes 196612
  242.6 32.6 %all-to-all-start.3 = ((bf16[128,2,128]{2,1,0:T(2,128)(2,1)}), bf16[128,2,128]{2,1,0:T(2,128)(2,1)S(1)}, u32[]{:S(2)}, u32[]{:S(2)}) async-start(bf16[128,2,128]{2,1,0:T(2,128)(2,1)} %reshape.160), calls=%async_computation.3 | async-start | bytes 131072 | tf_op jit(solution)/shard_map/all_to_all | solution.py:92
  256.9 32.1 %copy-start.2 = (s32[128]{0:T(128)S(1)}, s32[128]{0:T(128)}, u32[]{:S(2)}) copy-start(s32[128]{0:T(128)} %param.9) | copy-start | bytes 1540
  275.3 25.0 %all-to-all-start.2 = ((bf16[128,2,128]{2,1,0:T(2,128)(2,1)}), bf16[128,2,128]{2,1,0:T(2,128)(2,1)S(1)}, u32[]{:S(2)}, u32[]{:S(2)}) async-start(bf16[128,2,128]{2,1,0:T(2,128)(2,1)} %reshape.158), calls=%async_computation.2 | async-start | bytes 131072 | tf_op jit(solution)/shard_map/all_to_all | solution.py:91
  335.6 4.3 %collective-permute-start = (bf16[4,8,1024]{2,1,0:T(8,128)(2,1)S(1)}, bf16[4,8,1024]{2,1,0:T(8,128)(2,1)S(1)}, u32[]{:S(2)}, u32[]{:S(2)}) collective-permute-start(bf16[4,8,1024]{2,1,0:T(8,128)(2,1)S(1)} %fusion.76), channel_id=1, source_target_pairs={{0,1},{1,0},{2,3},{3,2},{4,5},{5,4},{6,7},{7,6},{8,9},{9,8},{10,11... | collective-permute-start | bytes 196616 | tf_op jit(solution)/shard_map/ppermute | solution.py:14
Sparse Core Ops, SparseCore 0:
  164.7 26.5 all-reduce.2
where the time goes:
time: 357 us; the launch traced here: 351 us
  matrix products  198 us (55%)
  starting transfers between devices  59.2 us (17%)
  local copies, waits for them, and re-layouts  43.4 us (12%)
  waiting for transfers between devices  34.3 us (10%)
  between operations  14.7 us (4%)
    psum x1, waiting for transfers between devices, on_device(): lax.psum(numer_im.astype(jnp.bfloat16), 'dist').astype(jnp.float32)  26.7 us
    unnamed x22, local copies, waits for them, and re-layouts  19.5 us
    dot_general x1, matrix products, on_device(): jnp.einsum('akq,qy->aky', spec_phase_re, sine, preferred_element_type=jnp...  16.9 us
    dot_general x1, matrix products, on_device(): jnp.einsum('aysk,syq->akq', imag_part, col_sin, preferred_element_type=jn...  16.8 us
    dot_general x1, matrix products, on_device(): jnp.einsum('aysk,syq->akq', real_part, col_sin, preferred_element_type=jn...  16.5 us
    dot_general x1, matrix products, on_device(): jnp.dot(flat, sine, preferred_element_type=jnp.float32)  16.1 us
    dot_general x1, matrix products, on_device(): jnp.einsum('akq,qy->aky', spec_phase_im, sine, preferred_element_type=jnp...  16.1 us
    dot_general x1, matrix products, on_device(): jnp.einsum('aysk,syq->akq', real_part, col_cos, preferred_element_type=jn...  16.1 us
  transfers between devices with their start and end apart: 6, of which 4 were waited for; matrix products, arithmetic and copies ran while one was open for 16% of the time, Pallas kernels for 0%

commit v1 on v0

--- a/solution.py
+++ b/solution.py
@@ -6,6 +6,11 @@
 
 absorb_ratio = 0.1
 regularizer = 0.05
+
+
+def summed_here(shard, name):
+    pieces = lax.all_gather(shard, name)
+    return jnp.sum(pieces, axis=0)
 
 
 def swapped(value, axis, bit):
@@ -75,7 +80,7 @@
     numer_im = jnp.sum(mine[None] * spec_im, axis=1)
     numer_re, numer_im = (
         lax.psum(numer_re.astype(jnp.bfloat16), "dist").astype(jnp.float32),
-        lax.psum(numer_im.astype(jnp.bfloat16), "dist").astype(jnp.float32),
+        summed_here(numer_im.astype(jnp.bfloat16), "dist").astype(jnp.float32),
     )
     spec_phase_re = (numer_re / denom).astype(jnp.bfloat16)
     spec_phase_im = (numer_im / denom).astype(jnp.bfloat16)

time: 357 us -> 342 us (0.958)
  waiting for transfers between devices: 34.3 us -> 16 us
    psum x1, waiting for transfers between devices: 26.7 us -> 8.46 us  [on_device(): lax.psum(numer_re.astype(jnp.bfloat16), 'dist').astype(jnp.float32)]
    unnamed x22 -> x20, local copies, waits for them, and re-layouts: 19.5 us -> 19.5 us
  transfers between devices with their start and end apart: 6 -> 6, of which waited for: 4 -> 4; matrix products, arithmetic and copies ran while one was open for 16% -> 22% of each run, Pallas kernels for 0% -> 0%
where the time goes in v1:
time: 342 us; the launch traced here: 335 us
  matrix products  199 us (58%)
  starting transfers between devices  59.4 us (17%)
  local copies, waits for them, and re-layouts  43.2 us (13%)
  waiting for transfers between devices  16 us (5%)
  between operations  14.7 us (4%)
    unnamed x20, local copies, waits for them, and re-layouts  19.5 us
    dot_general x1, matrix products, on_device(): jnp.einsum('aysk,syq->akq', imag_part, col_sin, preferred_element_type=jn...  17.5 us
    dot_general x1, matrix products, on_device(): jnp.einsum('akq,qy->aky', spec_phase_re, sine, preferred_element_type=jnp...  16.7 us
    dot_general x1, matrix products, on_device(): jnp.einsum('aysk,syq->akq', real_part, col_sin, preferred_element_type=jn...  16.6 us
    dot_general x1, matrix products, on_device(): jnp.einsum('aysk,syq->akq', real_part, col_cos, preferred_element_type=jn...  16.2 us
    dot_general x1, matrix products, on_device(): jnp.einsum('akq,qy->aky', spec_phase_im, cosine, preferred_element_type=j...  16.1 us
    dot_general x1, matrix products, on_device(): jnp.einsum('akq,qy->aky', spec_phase_im, sine, preferred_element_type=jnp...  16.1 us
    dot_general x1, matrix products, on_device(): jnp.dot(flat, sine, preferred_element_type=jnp.float32)  16.1 us
  transfers between devices with their start and end apart: 6, of which 4 were waited for; matrix products, arithmetic and copies ran while one was open for 22% of the time, Pallas kernels for 0%

profile of v1, /device:TPU:2, one launch (start us, length us, event | category | flops | bytes accessed | tf_op | source)
XLA Modules:
  0.0 335.4 jit_solution(17523488243073255542)
XLA Ops:
  7.4 16.1 %fusion.66 = bf16[8,8,1024]{2,1,0:T(8,128)(2,1)S(1)} fusion(bf16[64,1024]{1,0:T(8,128)(2,1)S(1)} %bitcast.133), kind=kOutput, calls=%fused_computation.56 | convolution fusion | flops 151126016 | bytes 262144 | tf_op jit(solution)/shard_map/dot_general | solution.py:57
  25.1 2.9 reshape.165
  28.0 16.0 %all-to-all-start.1 = ((bf16[128,2,256]{2,1,0:T(2,128)(2,1)}), bf16[128,2,256]{2,1,0:T(2,128)(2,1)S(1)}, u32[]{:S(2)}, u32[]{:S(2)}) async-start(bf16[128,2,256]{2,1,0:T(2,128)(2,1)} %reshape.165), calls=%async_computation.1 | async-start | bytes 262144 | tf_op jit(solution)/shard_map/all_to_all | solution.py:62
  44.0 16.0 %fusion.65 = bf16[8,8,1024]{2,1,0:T(8,128)(2,1)S(1)} fusion(bf16[64,1024]{1,0:T(8,128)(2,1)S(1)} %bitcast.134), kind=kOutput, calls=%fused_computation.55 | convolution fusion | flops 151060480 | bytes 262144 | tf_op jit(solution)/shard_map/dot_general | solution.py:56
  62.3 2.9 reshape.163
  65.2 13.8 %all-to-all-start = ((bf16[128,2,256]{2,1,0:T(2,128)(2,1)}), bf16[128,2,256]{2,1,0:T(2,128)(2,1)S(1)}, u32[]{:S(2)}, u32[]{:S(2)}) async-start(bf16[128,2,256]{2,1,0:T(2,128)(2,1)} %reshape.163), calls=%async_computation | async-start | bytes 262144 | tf_op jit(solution)/shard_map/all_to_all | solution.py:61
  79.1 3.5 %reshape.166 = bf16[1024,8,8]{2,1,0:T(8,128)(2,1)} reshape(bf16[128,2,256]{2,1,0:T(2,128)(2,1)S(1)} %all-to-all-done.1) | data formatting | bytes 262144
  82.6 4.3 %copy.30 = bf16[8,8,128,8]{3,2,1,0:T(8,128)(2,1)S(1)} copy(bf16[8,8,128,8]{1,0,3,2:T(8,128)(2,1)} %bitcast.137) | data formatting | bytes 262144 | tf_op jit(solution)/shard_map/reshape | solution.py:66
  86.9 3.6 %all-to-all-done = bf16[128,2,256]{2,1,0:T(2,128)(2,1)S(1)} async-done(((bf16[128,2,256]{2,1,0:T(2,128)(2,1)}), bf16[128,2,256]{2,1,0:T(2,128)(2,1)S(1)}, u32[]{:S(2)}, u32[]{:S(2)}) %all-to-all-start) | async-done | bytes 131104 | tf_op jit(solution)/shard_map/all_to_all | solution.py:61
  90.5 3.5 %reshape.164 = bf16[1024,8,8]{2,1,0:T(8,128)(2,1)} reshape(bf16[128,2,256]{2,1,0:T(2,128)(2,1)S(1)} %all-to-all-done) | data formatting | bytes 262144
  94.0 5.2 %copy.28 = bf16[8,8,128,8]{3,2,1,0:T(8,128)(2,1)} copy(bf16[8,8,128,8]{1,0,3,2:T(8,128)(2,1)} %bitcast.138) | data formatting | bytes 262144 | tf_op jit(solution)/shard_map/reshape | solution.py:65
  99.2 16.0 %fusion.39 = f32[8,8,1024]{2,1,0:T(8,128)S(1)} fusion(bf16[8,8,128,8]{3,2,1,0:T(8,128)(2,1)S(1)} %copy.30, s32[128,8]{0,1:T(8,128)S(1)} %multiply_add_fusion), kind=kOutput, calls=%fused_computation.42 | convolution fusion | flops 150994944 | bytes 397312 | tf_op jit(solution)/shard_map/aysk,syq->akq/dot_general | solution.py:71
  115.2 16.2 %fusion.36 = f32[8,8,1024]{2,1,0:T(8,128)S(1)} fusion(bf16[8,8,128,8]{3,2,1,0:T(8,128)(2,1)S(1)} %copy-done.1, s32[128,8]{0,1:T(8,128)S(1)} %multiply_add_fusion), kind=kOutput, calls=%fused_computation.41 | convolution fusion | flops 150994944 | bytes 397312 | tf_op jit(solution)/shard_map/aysk,syq->akq/dot_general | solution.py:67
  131.5 16.6 %fusion.48 = f32[8,8,1024]{2,1,0:T(8,128)S(1)} fusion(f32[8,8,1024]{2,1,0:T(8,128)S(1)} %fusion.39, bf16[8,8,128,8]{3,2,1,0:T(8,128)(2,1)S(1)} %copy-done.1, s32[128,8]{0,1:T(8,128)S(1)} %multiply_add_fusion), kind=kOutput, calls=%fused_computation.45 | convolution fusion | flops 151060480 | bytes 659456 | tf_op jit(solution)/shard_map/aysk,syq->akq/dot_general | solution.py:72
  148.0 17.5 %multiply_reduce_fusion.1 = (bf16[4,8,1024]{2,1,0:T(8,128)(2,1)}, bf16[4,8,1024]{2,1,0:T(8,128)(2,1)S(1)}) fusion(f32[2,8,1024]{2,1,0:T(8,128)S(1)} %constant_dynamic-slice_fusion, f32[8,8,1024]{2,1,0:T(8,128)S(1)} %fusion.48, f32[8,8,1024]{2,1,0:T(8,128)S(1)} %fusion.36, bf16[8,8,128,8]{3,2,1,0:T(8,128)(2,1)S(1)} %copy.30, s32[128,8]{0,1:T(8,128)S(1)} %multiply_add_fusion), kind=kOutput, calls=%fused_computation.66 | convolution fusion | flops 151257088 | bytes 856064 | tf_op jit(solution)/shard_map/aysk,syq->akq/dot_general | solution.py:68
  165.5 1.9 all-gather
  167.5 16.1 %fusion.16 = f32[4,8,1024]{2,1,0:T(8,128)S(1)} fusion(bf16[4,8,1024]{2,1,0:T(8,128)(2,1)S(1)} %reduce_sum.42, f32[8,1024]{1,0:T(8,128)S(1)} %broadcast_add_fusion), kind=kOutput, calls=%fused_computation.27 | convolution fusion | flops 83984384 | bytes 229376 | tf_op jit(solution)/shard_map/akq,qy->aky/dot_general | solution.py:89
  183.6 8.5 %all-reduce.2.cloned.1.call-done = bf16[4,8,1024]{2,1,0:T(8,128)(2,1)} async-done(((bf16[4,8,1024]{2,1,0:T(8,128)(2,1)}), bf16[4,8,1024]{2,1,0:T(8,128)(2,1)}) %all-reduce.2.cloned.1.call-update) | async-done | bytes 65552 | tf_op jit(solution)/shard_map/psum | solution.py:82
  192.0 16.7 %fusion.14 = f32[4,8,1024]{2,1,0:T(8,128)S(1)} fusion(bf16[4,8,1024]{2,1,0:T(8,128)(2,1)} %all-reduce.2.cloned.1.call-done, f32[8,1024]{1,0:T(8,128)S(1)} %broadcast_add_fusion), kind=kOutput, calls=%fused_computation.25 | convolution fusion | flops 83984384 | bytes 229376 | tf_op jit(solution)/shard_map/akq,qy->aky/dot_general | solution.py:93
  208.7 16.1 %fusion.79 = bf16[4,8,1024]{2,1,0:T(8,128)(2,1)S(1)} fusion(f32[4,8,1024]{2,1,0:T(8,128)S(1)} %fusion.14, bf16[4,8,1024]{2,1,0:T(8,128)(2,1)S(1)} %reduce_sum.42, f32[8,1024]{1,0:T(8,128)S(1)} %broadcast_add_fusion), kind=kOutput, calls=%fused_computation.61 | convolution fusion | flops 84049920 | bytes 294912 | tf_op jit(solution)/shard_map/akq,qy->aky/dot_general | solution.py:91
  225.5 1.7 reshape.169
  227.2 14.3 %all-to-all-start.3 = ((bf16[128,2,128]{2,1,0:T(2,128)(2,1)}), bf16[128,2,128]{2,1,0:T(2,128)(2,1)S(1)}, u32[]{:S(2)}, u32[]{:S(2)}) async-start(bf16[128,2,128]{2,1,0:T(2,128)(2,1)} %reshape.169), calls=%async_computation.3 | async-start | bytes 131072 | tf_op jit(solution)/shard_map/all_to_all | solution.py:97
  241.5 15.9 %fusion.82 = bf16[4,8,1024]{2,1,0:T(8,128)(2,1)S(1)} fusion(f32[4,8,1024]{2,1,0:T(8,128)S(1)} %fusion.16, bf16[4,8,1024]{2,1,0:T(8,128)(2,1)S(1)} %copy-done.4, f32[8,1024]{1,0:T(8,128)S(1)} %broadcast_add_fusion), kind=kOutput, calls=%fused_computation.62 | convolution fusion | flops 84049920 | bytes 294912 | tf_op jit(solution)/shard_map/akq,qy->aky/dot_general | solution.py:87
  259.8 13.8 %all-to-all-start.2 = ((bf16[128,2,128]{2,1,0:T(2,128)(2,1)}), bf16[128,2,128]{2,1,0:T(2,128)(2,1)S(1)}, u32[]{:S(2)}, u32[]{:S(2)}) async-start(bf16[128,2,128]{2,1,0:T(2,128)(2,1)} %reshape.167), calls=%async_computation.2 | async-start | bytes 131072 | tf_op jit(solution)/shard_map/all_to_all | solution.py:96
  274.8 4.9 %gather_fusion = bf16[4,1024,512]{2,1,0:T(8,128)(2,1)} fusion(bf16[4,1024,512]{2,1,0:T(8,128)(2,1)} %param.7, s32[1024]{0:T(1024)S(1)} %pad_clamp_fusion), kind=kCustom, calls=%fused_computation | custom fusion | bytes 8388624 | tf_op jit(solution)/shard_map/gather | solution.py:106
  281.0 2.1 copy.38
  283.0 1.8 all-to-all-done.2
  286.0 2.2 copy.36
  288.3 15.8 %fusion.57 = f32[4,8,1024]{2,1,0:T(8,128)S(1)} fusion(bf16[4,8,128,8]{3,2,1,0:T(8,128)(2,1)S(1)} %copy.36, s32[128,8]{0,1:T(8,128)S(1)} %multiply_add_fusion), kind=kOutput, calls=%fused_computation.51 | convolution fusion | flops 83886080 | bytes 200704 | tf_op jit(solution)/shard_map/aksy,skx->ayx/dot_general | solution.py:102
  304.1 16.0 %fusion.76 = bf16[4,8,1024]{2,1,0:T(8,128)(2,1)S(1)} fusion(f32[4,8,1024]{2,1,0:T(8,128)S(1)} %fusion.57, bf16[4,8,128,8]{3,2,1,0:T(8,128)(2,1)S(1)} %copy.38, s32[128,8]{0,1:T(8,128)S(1)} %multiply_add_fusion), kind=kOutput, calls=%fused_computation.60 | convolution fusion | flops 83951616 | bytes 266240 | tf_op jit(solution)/shard_map/aksy,skx->ayx/dot_general | solution.py:104
  322.3 2.2 collective-permute-done
  324.5 3.6 %fusion.86 = bf16[16,512]{1,0:T(8,128)(2,1)} fusion(bf16[4,1024,512]{2,1,0:T(8,128)(2,1)} %gather_fusion, bf16[4,8,1024]{2,1,0:T(8,128)(2,1)S(1)} %get-tuple-element.8, bf16[4,8,1024]{2,1,0:T(8,128)(2,1)S(1)} %get-tuple-element.7, s32[16]{0:T(128)S(1)} %iota_add_fusion, pred[16]{0:T(512)(128)(4,1)S(1)} %iota_compare_fusion.1), kind=kOutput, calls=%fused_computation.64 | convolution fusion | flops 69542912 | bytes 4341840 | tf_op jit(solution)/shard_map/ayx,axp->yp/dot_general | solution.py:114
  (39 shorter events, 12.9 us)
Async XLA Ops:
  6.5 0.9 copy-start
  28.0 37.2 %all-to-all-start.1 = ((bf16[128,2,256]{2,1,0:T(2,128)(2,1)}), bf16[128,2,256]{2,1,0:T(2,128)(2,1)S(1)}, u32[]{:S(2)}, u32[]{:S(2)}) async-start(bf16[128,2,256]{2,1,0:T(2,128)(2,1)} %reshape.165), calls=%async_computation.1 | async-start | bytes 262144 | tf_op jit(solution)/shard_map/all_to_all | solution.py:62
  44.0 16.2 %copy-start.3 = (f32[4]{0:T(128)S(1)}, f32[4]{0:T(128)}, u32[]{:S(2)}) copy-start(f32[4]{0:T(128)} %param.6) | copy-start | bytes 52
  60.0 5.2 %copy-start.5 = (s32[1,4]{1,0:T(1,128)S(1)}, s32[1,4]{1,0:T(1,128)}, u32[]{:S(2)}) copy-start(s32[1,4]{1,0:T(1,128)} %param.8) | copy-start | bytes 52
  65.2 25.3 %all-to-all-start = ((bf16[128,2,256]{2,1,0:T(2,128)(2,1)}), bf16[128,2,256]{2,1,0:T(2,128)(2,1)S(1)}, u32[]{:S(2)}, u32[]{:S(2)}) async-start(bf16[128,2,256]{2,1,0:T(2,128)(2,1)} %reshape.163), calls=%async_computation | async-start | bytes 262144 | tf_op jit(solution)/shard_map/all_to_all | solution.py:61
  79.0 113.0 %all-reduce.2.cloned.1.call-start = ((), (), s32[]{:S(2)}) async-start(), calls=%async_computation.4 | async-start | bytes 131072 | tf_op jit(solution)/shard_map/psum | solution.py:82
  99.2 16.1 %copy-start.1 = (bf16[8,8,128,8]{3,2,1,0:T(8,128)(2,1)S(1)}, bf16[8,8,128,8]{3,2,1,0:T(8,128)(2,1)}, u32[]{:S(2)}) copy-start(bf16[8,8,128,8]{3,2,1,0:T(8,128)(2,1)} %copy.28) | copy-start | bytes 393220
  208.7 32.8 %copy-start.4 = (bf16[4,8,1024]{2,1,0:T(8,128)(2,1)S(1)}, bf16[4,8,1024]{2,1,0:T(8,128)(2,1)}, u32[]{:S(2)}) copy-start(bf16[4,8,1024]{2,1,0:T(8,128)(2,1)} %all-reduce.2.cloned.1.call-done) | copy-start | bytes 196612
  227.2 32.6 %all-to-all-start.3 = ((bf16[128,2,128]{2,1,0:T(2,128)(2,1)}), bf16[128,2,128]{2,1,0:T(2,128)(2,1)S(1)}, u32[]{:S(2)}, u32[]{:S(2)}) async-start(bf16[128,2,128]{2,1,0:T(2,128)(2,1)} %reshape.169), calls=%async_computation.3 | async-start | bytes 131072 | tf_op jit(solution)/shard_map/all_to_all | solution.py:97
  241.5 32.2 %copy-start.2 = (s32[128]{0:T(128)S(1)}, s32[128]{0:T(128)}, u32[]{:S(2)}) copy-start(s32[128]{0:T(128)} %param.9) | copy-start | bytes 1540
  259.8 25.0 %all-to-all-start.2 = ((bf16[128,2,128]{2,1,0:T(2,128)(2,1)}), bf16[128,2,128]{2,1,0:T(2,128)(2,1)S(1)}, u32[]{:S(2)}, u32[]{:S(2)}) async-start(bf16[128,2,128]{2,1,0:T(2,128)(2,1)} %reshape.167), calls=%async_computation.2 | async-start | bytes 131072 | tf_op jit(solution)/shard_map/all_to_all | solution.py:96
  320.1 4.3 %collective-permute-start = (bf16[4,8,1024]{2,1,0:T(8,128)(2,1)S(1)}, bf16[4,8,1024]{2,1,0:T(8,128)(2,1)S(1)}, u32[]{:S(2)}, u32[]{:S(2)}) collective-permute-start(bf16[4,8,1024]{2,1,0:T(8,128)(2,1)S(1)} %fusion.76), channel_id=1, source_target_pairs={{0,1},{1,0},{2,3},{3,2},{4,5},{5,4},{6,7},{7,6},{8,9},{9,8},{10,11... | collective-permute-start | bytes 196616 | tf_op jit(solution)/shard_map/ppermute | solution.py:19
Sparse Core Ops, SparseCore 0:
  165.7 26.3 all-reduce.1
